TPU v7x, 256 devices: a whole 4x4x8 slice. The times are simulated.
256 devices in a mesh: ctx: 16 (over z, x_hi), fsdp: 16 (over x_lo, y, core).
Axes of the slice: x: 4 (x_hi: 2, x_lo: 2; x = x_hi * 2 + x_lo), y: 4, z: 8, core: 2. Of those that a mesh axis runs over, the one named last changes fastest.
Arguments:
- out_grad: bfloat16 [2048, 8192], P('ctx', 'fsdp'), may hold values from -6 to 6
- out_weight: bfloat16 [8192, 8192], P('ctx', 'fsdp'), may hold values from -0.0625 to 0.0625
- projections: bfloat16 [3, 2048, 8192], P(None, 'ctx', 'fsdp'), may hold values from -6 to 6
- short_filters: float32 [3, 3, 8192], P(None, None, 'fsdp'), may hold values from -3 to 3
- residues: float32 [16, 8192], P(None, 'fsdp'), may hold values from -0.06 to 0.06
- decay_rates: float32 [16, 8192], P(None, 'fsdp'), may hold values from 4.8828126e-05 to 0.05
Outputs:
- grad_weight: bfloat16 [8192, 8192], P('ctx', 'fsdp')
- grad_projections: bfloat16 [3, 2048, 8192], P(None, 'ctx', 'fsdp')
- grad_short: float32 [3, 3, 8192], P(None, None, 'fsdp')
- grad_residues: float32 [16, 8192], P(None, 'fsdp')
- grad_rates: float32 [16, 8192], P(None, 'fsdp')
All inputs are finite; a program needn't handle non-finite values.
Results may differ from a plain program's by a relative error of at most 0.005.
Values may be sent and summed in bfloat16 or wider, within the bound.
No kernel may reach another device: no remote copies, remote signals or barrier semaphores. Data moves between devices by JAX's collectives and lax.ppermute only.
A program may use at most 128 MiB of HBM per device.

v0:
```python
import math
import jax
import jax.numpy as jnp
from jax import lax
from jax.sharding import PartitionSpec as P


def from_behind(block, axis, distance):
    devices = range(lax.axis_size(axis))
    route = [(i - distance, i) for i in devices if i - distance in devices]
    return lax.ppermute(block, axis, route)


def carried_in(array, axis, combine, identity, reverse):
    devices, index = (lax.axis_size(axis), lax.axis_index(axis))
    everything = jax.tree.map(lambda part: lax.all_gather(part, axis), array)
    start = jax.tree.map(
        lambda part, zero: jnp.broadcast_to(jnp.asarray(zero, part.dtype), part.shape),
        array,
        identity,
    )

    def lap(k, before):
        at = devices - 1 - k if reverse else k
        reached = at > index if reverse else at < index
        new = combine(before, jax.tree.map(lambda part: part[at], everything))
        return jax.tree.map(lambda a, b: jnp.where(reached, a, b), new, before)

    return lax.fori_loop(0, devices, lap, start)


def link(earlier, later):
    return (earlier[0] * later[0], later[0] * earlier[1] + later[1])


def local_scan(decay, values):
    length = values.shape[0]
    piece_len = math.gcd(length, 32)
    block_count = length // piece_len
    grouped = values.reshape((block_count, piece_len) + values.shape[1:])
    running = jnp.zeros((block_count,) + decay.shape, jnp.float32)
    outputs = []
    for offset in range(piece_len):
        running = decay * running + grouped[:, offset]
        outputs.append(running)
    inner = jnp.stack(outputs, axis=1)
    jump = jnp.power(decay, float(piece_len))

    def carry_step(carry, final):
        return (jump * carry + final, carry)

    _, entering = lax.scan(carry_step, jnp.zeros(decay.shape, jnp.float32), inner[:, -1])
    steps_in = jnp.arange(piece_len, dtype=jnp.float32) + 1.0
    rising = jnp.power(decay[None], steps_in[:, None, None])
    whole = inner + rising[None] * entering[:, None]
    return whole.reshape((length,) + decay.shape)


def on_device(out_grad, out_weight, projections, short_filters, residues, decay_rates):
    panels = lax.all_gather(out_grad, "fsdp", axis=1, tiled=True)
    length = out_grad.shape[0]
    columns = panels
    grad_y = jnp.dot(
        columns,
        lax.all_gather(out_weight, "ctx", axis=0, tiled=True),
        preferred_element_type=jnp.float32,
    )
    taps = short_filters.shape[1]
    margin = taps - 1
    before = from_behind(projections[:, length - margin :, :], "ctx", 1)
    extended = jnp.concatenate([before, projections], axis=1).astype(jnp.float32)
    branches = short_filters[:, 0, None, :] * extended[:, margin : margin + length, :]
    for offset in range(1, taps):
        branches = (
            branches
            + short_filters[:, offset, None, :]
            * extended[:, margin - offset : margin - offset + length, :]
        )
    q_branch, k_branch, v_branch = (branches[0], branches[1], branches[2])
    product_kv = k_branch * v_branch
    decay = jnp.exp(-decay_rates)
    block_decay = jnp.exp(-decay_rates * float(length))
    positions = jnp.arange(length, dtype=jnp.float32)
    states_local = local_scan(decay, product_kv[:, None, :])
    identity = (jnp.ones_like(decay), jnp.zeros_like(decay))
    state_in = carried_in((block_decay, states_local[-1]), "ctx", link, identity, False)[1]
    rising = jnp.exp(-decay_rates[None] * (positions + 1.0)[:, None, None])
    states = states_local + rising * state_in[None]
    long_out = jnp.sum(residues[None] * states, axis=1)
    y_rounded = (q_branch * long_out).astype(jnp.bfloat16)
    grad_long = grad_y * q_branch
    grad_q = grad_y * long_out
    flipped = jnp.flip(grad_long, axis=0)
    adjoint_local = jnp.flip(local_scan(decay, residues[None] * flipped[:, None, :]), axis=0)
    adjoint_in = carried_in((block_decay, adjoint_local[0]), "ctx", link, identity, True)[1]
    falling = jnp.exp(-decay_rates[None] * (float(length) - positions)[:, None, None])
    adjoint = adjoint_local + falling * adjoint_in[None]
    grad_kv = jnp.sum(adjoint, axis=1)
    grad_res_part = jnp.sum(grad_long[:, None, :] * states, axis=0)
    previous = jnp.concatenate([state_in[None], states[:-1]], axis=0)
    grad_rate_part = -decay * jnp.sum(adjoint * previous, axis=0)
    grad_branches = jnp.stack([grad_q, grad_kv * v_branch, grad_kv * k_branch])
    after = from_behind(grad_branches[:, :margin, :], "ctx", -1)
    extended_back = jnp.concatenate([grad_branches, after], axis=1)
    grad_raw = short_filters[:, 0, None, :] * extended_back[:, 0:length, :]
    filter_terms = [jnp.sum(grad_branches * extended[:, margin : margin + length, :], axis=1)]
    for offset in range(1, taps):
        grad_raw = (
            grad_raw
            + short_filters[:, offset, None, :] * extended_back[:, offset : offset + length, :]
        )
        filter_terms.append(
            jnp.sum(
                grad_branches * extended[:, margin - offset : margin - offset + length, :], axis=1
            )
        )
    filter_part = jnp.stack(filter_terms, axis=1)
    grad_short, grad_res, grad_rate = lax.psum((filter_part, grad_res_part, grad_rate_part), "ctx")
    columns = panels
    grad_weight = lax.psum_scatter(
        lax.dot_general(
            columns, y_rounded, (((0,), (0,)), ((), ())), preferred_element_type=jnp.float32
        ),
        "ctx",
        scatter_dimension=0,
        tiled=True,
    )
    return (
        grad_weight.astype(jnp.bfloat16),
        grad_raw.astype(jnp.bfloat16),
        grad_short,
        grad_res,
        grad_rate,
    )


def solution(mesh):
    placed = (
        P("ctx", "fsdp"),
        P("ctx", "fsdp"),
        P(None, "ctx", "fsdp"),
        P(None, None, "fsdp"),
        P(None, "fsdp"),
        P(None, "fsdp"),
    )
    return jax.shard_map(
        on_device,
        mesh=mesh,
        in_specs=placed,
        out_specs=(
            P("ctx", "fsdp"),
            P(None, "ctx", "fsdp"),
            P(None, None, "fsdp"),
            P(None, "fsdp"),
            P(None, "fsdp"),
        ),
        check_vma=False,
    )
```

profile of v0, /device:TPU:1, one launch (start us, length us, event | category | flops | bytes accessed | tf_op | source)
XLA Modules:
  0.0 870.1 jit_solution(4104952560245108531)
XLA Ops:
  9.4 5.5 collective-permute-start
  18.4 39.6 %all-gather = f32[256,512]{1,0:T(8,128)} all-gather(f32[16,512]{1,0:T(8,128)S(1)} %get-tuple-element.508), channel_id=2, replica_groups=mesh['ctx'=16,'fsdp'=16] {'ctx'}, dimensions={0}, use_global_device_ids=true | all-gather | bytes 557056 | tf_op jit(solution)/shard_map/all_gather | solution.py:16
  58.0 1.8 broadcast_power_fusion
  68.7 119.7 %all-gather.6.cloned.1.call-done = bf16[8192,512]{1,0:T(8,128)(2,1)} async-done(((bf16[512,512]{1,0:T(8,128)(2,1)}), bf16[8192,512]{1,0:T(8,128)(2,1)}) %all-gather.6.cloned.1.call-update) | async-done | bytes 8388624 | tf_op jit(solution)/shard_map/all_gather | solution.py:65
  188.4 5.3 fusion.8
  239.3 1.7 constant_dynamic-update-slice_fusion.37
  247.6 1.7 constant_dynamic-update-slice_fusion.32
  254.9 1.7 constant_dynamic-update-slice_fusion.31
  265.3 5.6 while.58
  270.9 7.2 multiply_add_fusion.1
  280.1 2.0 copy-done.5
  282.1 32.5 %all_gather.22 = f32[16,16,512]{2,1,0:T(8,128)S(1)} all-gather(f32[1,16,512]{2,1,0:T(8,128)S(1)} %slice.365), channel_id=1, replica_groups=mesh['ctx'=16,'fsdp'=16] {'ctx'}, dimensions={0}, use_global_device_ids=true | all-gather | bytes 557056 | tf_op jit(solution)/shard_map/all_gather | solution.py:16
  314.7 12.7 %while.57 = (s32[]{:T(128)}, f32[16,512]{1,0:T(8,128)S(1)}, s32[]{:T(128)}, f32[16,16,512]{2,1,0:T(8,128)}, f32[16,16,512]{2,1,0:T(8,128)S(1)}, /*index=5*/s32[]{:T(128)}, s32[]{:T(128)}) while((s32[]{:T(128)}, f32[16,512]{1,0:T(8,128)S(1)}, s32[]{:T(128)}, f32[16,16,512]{2,1,0:T(8,128)}, f32[16,16,512]{2,1,0:T(8,128)S(1)}, ...), condition=%wide.region_3.4_spmd.clone, body=%wide.region_2.3_spmd.clone.sunk | while | flops 32772 | bytes 131173 | solution.py:29
  327.4 2.6 copy.25
  330.1 2.1 copy-done.3
  332.1 34.7 %all_gather.25 = f32[16,16,512]{2,1,0:T(8,128)S(1)} all-gather(f32[1,16,512]{2,1,0:T(8,128)S(1)} %slice.398), channel_id=1, replica_groups=mesh['ctx'=16,'fsdp'=16] {'ctx'}, dimensions={0}, use_global_device_ids=true | all-gather | bytes 557056 | tf_op jit(solution)/shard_map/all_gather | solution.py:16
  366.9 12.8 %while.59 = (s32[]{:T(128)}, f32[16,512]{1,0:T(8,128)S(1)}, s32[]{:T(128)}, f32[16,16,512]{2,1,0:T(8,128)}, f32[16,16,512]{2,1,0:T(8,128)S(1)}, /*index=5*/s32[]{:T(128)}, s32[]{:T(128)}, s32[]{:T(128)}, s32[]{:T(128)}) while((s32[]{:T(128)}, f32[16,512]{1,0:T(8,128)S(1)}, s32[]{:T(128)}, f32[16,16,512]{2,1,0:T(8,128)}, ...), condition=%wide.region_9.10_spmd.clone, body=%wide.region_8.9_spmd.clone.sunk | while | flops 32776 | bytes 131235 | solution.py:29
  379.7 3.1 slice_add_fusion
  383.2 2.3 fusion.2
  385.8 2.5 multiply_reduce_fusion
  390.6 4.0 collective-permute-done.1
  396.7 8.2 convolution_bitcast_fusion
  404.8 152.6 %all-reduce.3.cloned.1.call-done = (f32[3,3,512]{2,0,1:T(4,128)}, f32[16,512]{1,0:T(8,128)}, f32[16,512]{1,0:T(8,128)}) async-done(((f32[3,3,512]{2,0,1:T(4,128)}, f32[16,512]{1,0:T(8,128)}, f32[16,512]{1,0:T(8,128)}), (f32[3,3,512]{2,0,1:T(4,128)}, f32[16,512]{1,0:T(8,128)}, f32[16,512]{1,0:T(8,128)})) %all-reduce.3.cloned.1.call-update) | async-done | bytes 83984 | tf_op jit(solution)/shard_map/psum | solution.py:118
  558.8 299.8 %reduce-scatter.2.cloned.1.call-done = f32[512,512]{0,1:T(8,128)} async-done(((f32[8192,512]{0,1:T(8,128)}), f32[512,512]{0,1:T(8,128)}) %reduce-scatter.2.cloned.1.call-update) | async-done | bytes 1048592 | tf_op jit(solution)/shard_map/reduce_scatter | solution.py:120
  (296 shorter events, 124.1 us)
Async XLA Ops:
  7.2 60.9 %all-gather.4.cloned.1.call-start = ((), (), s32[]{:S(2)}) async-start(), calls=%async_computation.1 | async-start | bytes 2228224 | tf_op jit(solution)/shard_map/all_gather | solution.py:60
  7.9 180.5 %all-gather.6.cloned.1.call-start = ((), (), s32[]{:S(2)}) async-start(), calls=%async_computation.3 | async-start | bytes 8912896 | tf_op jit(solution)/shard_map/all_gather | solution.py:65
  8.6 548.8 %all-reduce.3.cloned.1.call-start = ((), (), s32[]{:S(2)}) async-start(), calls=%async_computation.4 | async-start | bytes 180224 | tf_op jit(solution)/shard_map/psum | solution.py:118
  9.4 50.9 %collective-permute-start = (bf16[3,2,512]{2,1,0:T(2,128)(2,1)S(1)}, bf16[3,2,512]{2,1,0:T(2,128)(2,1)S(1)}, u32[]{:S(2)}, u32[]{:S(2)}) collective-permute-start(bf16[3,2,512]{2,1,0:T(2,128)(2,1)S(1)} %slice.248), channel_id=1, source_target_pairs={{0,16},{16,32},{32,48},{48,64},{64,80},{80,96},{96,112},{112,128},... | collective-permute-start | bytes 18440 | tf_op jit(solution)/shard_map/ppermute | solution.py:11
  17.0 44.8 %copy-start.40 = (f32[3,512]{1,0:T(4,128)}, f32[3,512]{1,0:T(4,128)S(1)}, u32[]{:S(2)}) copy-start(f32[3,512]{1,0:T(4,128)S(1)} %get-tuple-element.514) | copy-start | bytes 18436
  17.0 44.9 %copy-start.42 = (f32[3,512]{1,0:T(4,128)}, f32[3,512]{1,0:T(4,128)S(1)}, u32[]{:S(2)}) copy-start(f32[3,512]{1,0:T(4,128)S(1)} %get-tuple-element.515) | copy-start | bytes 18436
  68.0 128.1 %copy-start.33 = (f32[16,512]{1,0:T(8,128)S(1)}, f32[16,512]{1,0:T(8,128)}, u32[]{:S(2)}) copy-start(f32[16,512]{1,0:T(8,128)} %param.18) | copy-start | bytes 98308
  223.0 24.5 %copy-start.8 = (f32[4,1,1,512]{3,0,1,2:T(4,128)S(1)}, f32[4,1,1,512]{3,0,1,2:T(4,128)}, u32[]{:S(2)}) copy-start(f32[4,1,1,512]{3,0,1,2:T(4,128)} %copy-done.7) | copy-start | bytes 24580
  224.7 24.6 %copy-start.14 = (f32[4,1,1,512]{3,0,1,2:T(4,128)S(1)}, f32[4,1,1,512]{3,0,1,2:T(4,128)}, u32[]{:S(2)}) copy-start(f32[4,1,1,512]{3,0,1,2:T(4,128)} %copy-done.13) | copy-start | bytes 24580
  226.3 23.8 %copy-start.20 = (f32[4,1,1,512]{3,0,1,2:T(4,128)S(1)}, f32[4,1,1,512]{3,0,1,2:T(4,128)}, u32[]{:S(2)}) copy-start(f32[4,1,1,512]{3,0,1,2:T(4,128)} %copy-done.19) | copy-start | bytes 24580
  226.3 24.6 %copy-start.24 = (f32[4,1,1,512]{3,0,1,2:T(4,128)S(1)}, f32[4,1,1,512]{3,0,1,2:T(4,128)}, u32[]{:S(2)}) copy-start(f32[4,1,1,512]{3,0,1,2:T(4,128)} %copy-done.23) | copy-start | bytes 24580
  228.0 23.7 %copy-start.28 = (f32[4,1,1,512]{3,0,1,2:T(4,128)S(1)}, f32[4,1,1,512]{3,0,1,2:T(4,128)}, u32[]{:S(2)}) copy-start(f32[4,1,1,512]{3,0,1,2:T(4,128)} %copy-done.27) | copy-start | bytes 24580
  229.5 22.9 %copy-start.30 = (f32[4,1,1,512]{3,0,1,2:T(4,128)S(1)}, f32[4,1,1,512]{3,0,1,2:T(4,128)}, u32[]{:S(2)}) copy-start(f32[4,1,1,512]{3,0,1,2:T(4,128)} %copy-done.29) | copy-start | bytes 24580
  229.5 23.7 %copy-start.36 = (f32[4,1,1,512]{3,0,1,2:T(4,128)S(1)}, f32[4,1,1,512]{3,0,1,2:T(4,128)}, u32[]{:S(2)}) copy-start(f32[4,1,1,512]{3,0,1,2:T(4,128)} %copy-done.35) | copy-start | bytes 24580
  231.2 22.8 %copy-start.47 = (f32[4,1,1,512]{3,0,1,2:T(4,128)S(1)}, f32[4,1,1,512]{3,0,1,2:T(4,128)}, u32[]{:S(2)}) copy-start(f32[4,1,1,512]{3,0,1,2:T(4,128)} %copy-done.46) | copy-start | bytes 24580
  237.7 20.9 %copy-start.10 = (f32[4,1,1,512]{3,0,1,2:T(4,128)S(1)}, f32[4,1,1,512]{3,0,1,2:T(4,128)}, u32[]{:S(2)}) copy-start(f32[4,1,1,512]{3,0,1,2:T(4,128)} %copy-done.9) | copy-start | bytes 24580
  239.3 20.1 %copy-start.12 = (f32[4,1,1,512]{3,0,1,2:T(4,128)S(1)}, f32[4,1,1,512]{3,0,1,2:T(4,128)}, u32[]{:S(2)}) copy-start(f32[4,1,1,512]{3,0,1,2:T(4,128)} %copy-done.11) | copy-start | bytes 24580
  239.3 20.8 %copy-start.18 = (f32[4,1,1,512]{3,0,1,2:T(4,128)S(1)}, f32[4,1,1,512]{3,0,1,2:T(4,128)}, u32[]{:S(2)}) copy-start(f32[4,1,1,512]{3,0,1,2:T(4,128)} %copy-done.17) | copy-start | bytes 24580
  241.0 19.8 %copy-start.22 = (f32[4,1,1,512]{3,0,1,2:T(4,128)S(1)}, f32[4,1,1,512]{3,0,1,2:T(4,128)}, u32[]{:S(2)}) copy-start(f32[4,1,1,512]{3,0,1,2:T(4,128)} %copy-done.21) | copy-start | bytes 24580
  242.6 19.7 %copy-start.32 = (f32[4,1,1,512]{3,0,1,2:T(4,128)S(1)}, f32[4,1,1,512]{3,0,1,2:T(4,128)}, u32[]{:S(2)}) copy-start(f32[4,1,1,512]{3,0,1,2:T(4,128)} %copy-done.31) | copy-start | bytes 24580
  327.4 52.3 %copy-start.15 = (f32[16,512]{1,0:T(8,128)S(1)}, f32[16,512]{1,0:T(8,128)}, u32[]{:S(2)}) copy-start(f32[16,512]{1,0:T(8,128)} %get-tuple-element.504) | copy-start | bytes 98308
  327.4 52.3 %copy-start.51 = (f32[128]{0:T(128)S(1)}, f32[128]{0:T(128)}, u32[]{:S(2)}) copy-start(f32[128]{0:T(128)} %iota_add_fusion) | copy-start | bytes 1540
  388.5 6.1 collective-permute-start.1
  396.6 462.0 %reduce-scatter.2.cloned.1.call-start = ((), (), s32[]{:S(2)}) async-start(), calls=%async_computation.2 | async-start | bytes 17825792 | tf_op jit(solution)/shard_map/reduce_scatter | solution.py:120
  (35 other events, 215.9 us)
Sparse Core Ops, SparseCore 0:
  9.8 41.2 all-gather.3
  53.7 134.6 all-gather.5
  396.7 160.7 all-reduce.2
  561.4 297.0 reduce-scatter.1
where the time goes:
time: 874 us; the launch traced here: 870 us
  waiting for transfers between devices  578 us (66%)
  other arithmetic  127 us (15%)
  blocking collectives  107 us (12%)
  local copies, waits for them, and re-layouts  21.9 us (3%)
  between operations  14.8 us (2%)
  matrix products  13.5 us (2%)
    reduce_scatter x1, waiting for transfers between devices, on_device(): lax.psum_scatter(lax.dot_general(columns, y_rounded, (((0,), (0,)), ((),...  300 us
    psum x1, waiting for transfers between devices, on_device(): lax.psum((filter_part, grad_res_part, grad_rate_part), 'ctx')  153 us
    all_gather x1, waiting for transfers between devices, on_device(): lax.all_gather(out_weight, 'ctx', axis=0, tiled=True)  120 us
    all_gather x3, blocking collectives, carried_in(): everything = jax.tree.map(lambda part: lax.all_gather(part, axis), array)  107 us
    unnamed x62, other arithmetic  68.5 us
    select_n x32, other arithmetic, lap(): return jax.tree.map(lambda a, b: jnp.where(reached, a, b), new, before)  24.7 us
  transfers between devices with their start and end apart: 6, of which 4 were waited for; matrix products, arithmetic and copies ran while one was open for 3% of the time, Pallas kernels for 0%

commit v1 on v0

--- a/solution.py
+++ b/solution.py
@@ -3,6 +3,13 @@
 import jax.numpy as jnp
 from jax import lax
 from jax.sharding import PartitionSpec as P
+
+
+def _get_plane(frame_in):
+    mid_arr = jnp.concatenate(
+        lax.all_to_all(jnp.stack([frame_in] * lax.axis_size("ctx"), 0), "ctx", 0, 0), 0
+    )
+    return mid_arr
 
 
 def from_behind(block, axis, distance):
@@ -60,11 +67,7 @@
     panels = lax.all_gather(out_grad, "fsdp", axis=1, tiled=True)
     length = out_grad.shape[0]
     columns = panels
-    grad_y = jnp.dot(
-        columns,
-        lax.all_gather(out_weight, "ctx", axis=0, tiled=True),
-        preferred_element_type=jnp.float32,
-    )
+    grad_y = jnp.dot(columns, _get_plane(out_weight), preferred_element_type=jnp.float32)
     taps = short_filters.shape[1]
     margin = taps - 1
     before = from_behind(projections[:, length - margin :, :], "ctx", 1)

time: 874 us -> 948 us (1.085)
  blocking collectives: 107 us -> 283 us
  waiting for transfers between devices: 578 us -> 463 us
  starting transfers between devices: 7.04 us -> 18 us
    all_gather x3, blocking collectives: 107 us -> 283 us  [carried_in(): everything = jax.tree.map(lambda part: lax.all_gather(part, axis), array)]
    all_gather x1 -> x0, waiting for transfers between devices: 120 us -> none  [on_device(): lax.all_gather(out_weight, 'ctx', axis=0, tiled=True)]
    all_to_all x0 -> x1, starting transfers between devices: none -> 11.8 us  [_get_plane(): lax.all_to_all(jnp.stack([frame_in] * lax.axis_size('ctx'), 0), 'ctx', 0, 0)]
  transfers between devices with their start and end apart: 6 -> 6, of which waited for: 4 -> 3; matrix products, arithmetic and copies ran while one was open for 3% -> 2% of each run, Pallas kernels for 0% -> 0%
where the time goes in v1:
time: 948 us; the launch traced here: 944 us
  waiting for transfers between devices  463 us (49%)
  blocking collectives  283 us (30%)
  other arithmetic  126 us (13%)
  local copies, waits for them, and re-layouts  25.5 us (3%)
  starting transfers between devices  18 us (2%)
  between operations  14.8 us (2%)
  matrix products  13.5 us (1%)
    reduce_scatter x1, waiting for transfers between devices, on_device(): lax.psum_scatter(lax.dot_general(columns, y_rounded, (((0,), (0,)), ((),...  300 us
    all_gather x3, blocking collectives, carried_in(): everything = jax.tree.map(lambda part: lax.all_gather(part, axis), array)  283 us
    psum x1, waiting for transfers between devices, on_device(): lax.psum((filter_part, grad_res_part, grad_rate_part), 'ctx')  159 us
    unnamed x62, other arithmetic  68.4 us
    select_n x32, other arithmetic, lap(): return jax.tree.map(lambda a, b: jnp.where(reached, a, b), new, before)  24.7 us
  transfers between devices with their start and end apart: 6, of which 3 were waited for; matrix products, arithmetic and copies ran while one was open for 2% of the time, Pallas kernels for 0%

profile of v1, /device:TPU:1, one launch (start us, length us, event | category | flops | bytes accessed | tf_op | source)
XLA Modules:
  0.0 944.1 jit_solution(2859764580392363595)
XLA Ops:
  7.2 5.2 stack.19
  12.3 11.8 %all-to-all-start = ((bf16[16,512,512]{2,1,0:T(8,128)(2,1)}), bf16[16,512,512]{2,1,0:T(8,128)(2,1)}, u32[]{:S(2)}, u32[]{:S(2)}) async-start(bf16[16,512,512]{2,1,0:T(8,128)(2,1)} %stack.19), calls=%async_computation.1 | async-start | bytes 16777216 | tf_op jit(solution)/shard_map/all_to_all | solution.py:10
  24.2 4.7 collective-permute-start
  30.9 214.9 %all-gather = f32[256,512]{1,0:T(8,128)} all-gather(f32[16,512]{1,0:T(8,128)S(1)} %get-tuple-element.508), channel_id=2, replica_groups=mesh['ctx'=16,'fsdp'=16] {'ctx'}, dimensions={0}, use_global_device_ids=true | all-gather | bytes 557056 | tf_op jit(solution)/shard_map/all_gather | solution.py:23
  245.8 1.8 broadcast_power_fusion
  255.3 5.3 fusion.8
  314.4 1.7 constant_dynamic-update-slice_fusion.32
  321.7 1.7 constant_dynamic-update-slice_fusion.31
  332.1 5.6 while.58
  337.7 7.2 multiply_add_fusion.1
  346.9 2.0 copy-done.5
  349.0 35.9 %all_gather.19 = f32[16,16,512]{2,1,0:T(8,128)S(1)} all-gather(f32[1,16,512]{2,1,0:T(8,128)S(1)} %slice.365), channel_id=1, replica_groups=mesh['ctx'=16,'fsdp'=16] {'ctx'}, dimensions={0}, use_global_device_ids=true | all-gather | bytes 557056 | tf_op jit(solution)/shard_map/all_gather | solution.py:23
  384.8 12.7 %while.57 = (s32[]{:T(128)}, f32[16,512]{1,0:T(8,128)S(1)}, s32[]{:T(128)}, f32[16,16,512]{2,1,0:T(8,128)}, f32[16,16,512]{2,1,0:T(8,128)S(1)}, /*index=5*/s32[]{:T(128)}, s32[]{:T(128)}) while((s32[]{:T(128)}, f32[16,512]{1,0:T(8,128)S(1)}, s32[]{:T(128)}, f32[16,16,512]{2,1,0:T(8,128)}, f32[16,16,512]{2,1,0:T(8,128)S(1)}, ...), condition=%wide.region_3.4_spmd.clone, body=%wide.region_2.3_spmd.clone.sunk | while | flops 32772 | bytes 131173 | solution.py:36
  397.6 2.6 copy.25
  400.2 2.1 copy-done.3
  402.3 32.0 %all_gather.21 = f32[16,16,512]{2,1,0:T(8,128)S(1)} all-gather(f32[1,16,512]{2,1,0:T(8,128)S(1)} %slice.398), channel_id=1, replica_groups=mesh['ctx'=16,'fsdp'=16] {'ctx'}, dimensions={0}, use_global_device_ids=true | all-gather | bytes 557056 | tf_op jit(solution)/shard_map/all_gather | solution.py:23
  434.3 12.8 %while.59 = (s32[]{:T(128)}, f32[16,512]{1,0:T(8,128)S(1)}, s32[]{:T(128)}, f32[16,16,512]{2,1,0:T(8,128)}, f32[16,16,512]{2,1,0:T(8,128)S(1)}, /*index=5*/s32[]{:T(128)}, s32[]{:T(128)}, s32[]{:T(128)}, s32[]{:T(128)}) while((s32[]{:T(128)}, f32[16,512]{1,0:T(8,128)S(1)}, s32[]{:T(128)}, f32[16,16,512]{2,1,0:T(8,128)}, ...), condition=%wide.region_9.10_spmd.clone, body=%wide.region_8.9_spmd.clone.sunk | while | flops 32776 | bytes 131235 | solution.py:36
  447.1 3.1 slice_add_fusion
  450.6 2.3 fusion.2
  453.2 2.5 multiply_reduce_fusion
  458.0 4.0 collective-permute-done.1
  464.1 8.2 convolution_bitcast_fusion
  472.3 159.0 %all-reduce.3.cloned.1.call-done = (f32[3,3,512]{2,0,1:T(4,128)}, f32[16,512]{1,0:T(8,128)}, f32[16,512]{1,0:T(8,128)}) async-done(((f32[3,3,512]{2,0,1:T(4,128)}, f32[16,512]{1,0:T(8,128)}, f32[16,512]{1,0:T(8,128)}), (f32[3,3,512]{2,0,1:T(4,128)}, f32[16,512]{1,0:T(8,128)}, f32[16,512]{1,0:T(8,128)})) %all-reduce.3.cloned.1.call-update) | async-done | bytes 83984 | tf_op jit(solution)/shard_map/psum | solution.py:121
  632.6 299.9 %reduce-scatter.2.cloned.1.call-done = f32[512,512]{0,1:T(8,128)} async-done(((f32[8192,512]{0,1:T(8,128)}), f32[512,512]{0,1:T(8,128)}) %reduce-scatter.2.cloned.1.call-update) | async-done | bytes 1048592 | tf_op jit(solution)/shard_map/reduce_scatter | solution.py:123
  (302 shorter events, 120.8 us)
Async XLA Ops:
  12.3 242.4 %all-to-all-start = ((bf16[16,512,512]{2,1,0:T(8,128)(2,1)}), bf16[16,512,512]{2,1,0:T(8,128)(2,1)}, u32[]{:S(2)}, u32[]{:S(2)}) async-start(bf16[16,512,512]{2,1,0:T(8,128)(2,1)} %stack.19), calls=%async_computation.1 | async-start | bytes 16777216 | tf_op jit(solution)/shard_map/all_to_all | solution.py:10
  24.1 230.6 %all-gather.3.cloned.1.call-start = ((), (), s32[]{:S(2)}) async-start(), calls=%async_computation.2 | async-start | bytes 2228224 | tf_op jit(solution)/shard_map/all_gather | solution.py:67
  24.2 224.0 %collective-permute-start = (bf16[3,2,512]{2,1,0:T(2,128)(2,1)S(1)}, bf16[3,2,512]{2,1,0:T(2,128)(2,1)S(1)}, u32[]{:S(2)}, u32[]{:S(2)}) collective-permute-start(bf16[3,2,512]{2,1,0:T(2,128)(2,1)S(1)} %slice.248), channel_id=1, source_target_pairs={{0,16},{16,32},{32,48},{48,64},{64,80},{80,96},{96,112},{112,128},... | collective-permute-start | bytes 18440 | tf_op jit(solution)/shard_map/ppermute | solution.py:18
  28.9 602.4 %all-reduce.3.cloned.1.call-start = ((), (), s32[]{:S(2)}) async-start(), calls=%async_computation.4 | async-start | bytes 180224 | tf_op jit(solution)/shard_map/psum | solution.py:121
  30.2 218.5 %copy-start.42 = (f32[3,512]{1,0:T(4,128)}, f32[3,512]{1,0:T(4,128)S(1)}, u32[]{:S(2)}) copy-start(f32[3,512]{1,0:T(4,128)S(1)} %get-tuple-element.514) | copy-start | bytes 18436
  30.2 218.5 %copy-start.44 = (f32[3,512]{1,0:T(4,128)}, f32[3,512]{1,0:T(4,128)S(1)}, u32[]{:S(2)}) copy-start(f32[3,512]{1,0:T(4,128)S(1)} %get-tuple-element.515) | copy-start | bytes 18436
  290.0 24.5 %copy-start.8 = (f32[4,1,1,512]{3,0,1,2:T(4,128)S(1)}, f32[4,1,1,512]{3,0,1,2:T(4,128)}, u32[]{:S(2)}) copy-start(f32[4,1,1,512]{3,0,1,2:T(4,128)} %copy-done.7) | copy-start | bytes 24580
  291.6 24.5 %copy-start.14 = (f32[4,1,1,512]{3,0,1,2:T(4,128)S(1)}, f32[4,1,1,512]{3,0,1,2:T(4,128)}, u32[]{:S(2)}) copy-start(f32[4,1,1,512]{3,0,1,2:T(4,128)} %copy-done.13) | copy-start | bytes 24580
  293.2 23.7 %copy-start.20 = (f32[4,1,1,512]{3,0,1,2:T(4,128)S(1)}, f32[4,1,1,512]{3,0,1,2:T(4,128)}, u32[]{:S(2)}) copy-start(f32[4,1,1,512]{3,0,1,2:T(4,128)} %copy-done.19) | copy-start | bytes 24580
  293.2 24.5 %copy-start.25 = (f32[4,1,1,512]{3,0,1,2:T(4,128)S(1)}, f32[4,1,1,512]{3,0,1,2:T(4,128)}, u32[]{:S(2)}) copy-start(f32[4,1,1,512]{3,0,1,2:T(4,128)} %copy-done.24) | copy-start | bytes 24580
  294.9 23.6 %copy-start.29 = (f32[4,1,1,512]{3,0,1,2:T(4,128)S(1)}, f32[4,1,1,512]{3,0,1,2:T(4,128)}, u32[]{:S(2)}) copy-start(f32[4,1,1,512]{3,0,1,2:T(4,128)} %copy-done.28) | copy-start | bytes 24580
  296.5 22.8 %copy-start.31 = (f32[4,1,1,512]{3,0,1,2:T(4,128)S(1)}, f32[4,1,1,512]{3,0,1,2:T(4,128)}, u32[]{:S(2)}) copy-start(f32[4,1,1,512]{3,0,1,2:T(4,128)} %copy-done.30) | copy-start | bytes 24580
  296.5 23.6 %copy-start.37 = (f32[4,1,1,512]{3,0,1,2:T(4,128)S(1)}, f32[4,1,1,512]{3,0,1,2:T(4,128)}, u32[]{:S(2)}) copy-start(f32[4,1,1,512]{3,0,1,2:T(4,128)} %copy-done.36) | copy-start | bytes 24580
  298.1 22.8 %copy-start.49 = (f32[4,1,1,512]{3,0,1,2:T(4,128)S(1)}, f32[4,1,1,512]{3,0,1,2:T(4,128)}, u32[]{:S(2)}) copy-start(f32[4,1,1,512]{3,0,1,2:T(4,128)} %copy-done.48) | copy-start | bytes 24580
  304.6 20.9 %copy-start.10 = (f32[4,1,1,512]{3,0,1,2:T(4,128)S(1)}, f32[4,1,1,512]{3,0,1,2:T(4,128)}, u32[]{:S(2)}) copy-start(f32[4,1,1,512]{3,0,1,2:T(4,128)} %copy-done.9) | copy-start | bytes 24580
  306.2 20.0 %copy-start.12 = (f32[4,1,1,512]{3,0,1,2:T(4,128)S(1)}, f32[4,1,1,512]{3,0,1,2:T(4,128)}, u32[]{:S(2)}) copy-start(f32[4,1,1,512]{3,0,1,2:T(4,128)} %copy-done.11) | copy-start | bytes 24580
  306.2 20.7 %copy-start.18 = (f32[4,1,1,512]{3,0,1,2:T(4,128)S(1)}, f32[4,1,1,512]{3,0,1,2:T(4,128)}, u32[]{:S(2)}) copy-start(f32[4,1,1,512]{3,0,1,2:T(4,128)} %copy-done.17) | copy-start | bytes 24580
  307.9 19.8 %copy-start.23 = (f32[4,1,1,512]{3,0,1,2:T(4,128)S(1)}, f32[4,1,1,512]{3,0,1,2:T(4,128)}, u32[]{:S(2)}) copy-start(f32[4,1,1,512]{3,0,1,2:T(4,128)} %copy-done.22) | copy-start | bytes 24580
  309.5 18.9 %copy-start.27 = (f32[4,1,1,512]{3,0,1,2:T(4,128)S(1)}, f32[4,1,1,512]{3,0,1,2:T(4,128)}, u32[]{:S(2)}) copy-start(f32[4,1,1,512]{3,0,1,2:T(4,128)} %copy-done.26) | copy-start | bytes 24580
  309.5 19.7 %copy-start.33 = (f32[4,1,1,512]{3,0,1,2:T(4,128)S(1)}, f32[4,1,1,512]{3,0,1,2:T(4,128)}, u32[]{:S(2)}) copy-start(f32[4,1,1,512]{3,0,1,2:T(4,128)} %copy-done.32) | copy-start | bytes 24580
  397.5 49.6 %copy-start.15 = (f32[16,512]{1,0:T(8,128)S(1)}, f32[16,512]{1,0:T(8,128)}, u32[]{:S(2)}) copy-start(f32[16,512]{1,0:T(8,128)} %get-tuple-element.504) | copy-start | bytes 98308
  397.6 49.6 %copy-start.54 = (f32[128]{0:T(128)S(1)}, f32[128]{0:T(128)}, u32[]{:S(2)}) copy-start(f32[128]{0:T(128)} %iota_add_fusion) | copy-start | bytes 1540
  455.9 6.1 collective-permute-start.1
  464.0 468.5 %reduce-scatter.2.cloned.1.call-start = ((), (), s32[]{:S(2)}) async-start(), calls=%async_computation.3 | async-start | bytes 17825792 | tf_op jit(solution)/shard_map/reduce_scatter | solution.py:123
  (38 other events, 248.6 us)
Sparse Core Ops, SparseCore 0:
  29.0 36.3 all-gather.2
  464.1 167.1 all-reduce.2
  635.4 297.0 reduce-scatter.1
